TPU v7x, 512 devices: a whole 4x8x8 slice. The times are simulated.
512 devices in a mesh: row: 16 (over y_hi, x), col: 32 (over z, y_lo, core).
Axes of the slice: x: 4, y: 8 (y_hi: 4, y_lo: 2; y = y_hi * 2 + y_lo), z: 8, core: 2. Of those that a mesh axis runs over, the one named last changes fastest.
Arguments:
- query: bfloat16 [16384, 1024], P(('row', 'col')), may hold values from -0.5375 to 0.5375
- passage: bfloat16 [16384, 1024], P(('row', 'col')), may hold values from -0.43 to 0.43
- positive: int32 [512, 32], P(('row', 'col')), may hold values from 0 to 31, each once within a row
Outputs:
- loss_value: float32 [], replicated
- grad_query: bfloat16 [16384, 1024], P(('row', 'col'))
- grad_passage: bfloat16 [16384, 1024], P(('row', 'col'))
Inputs may be any that keep to these rules, and one draw needn't show every extreme that they name: Each row of positive names every position 0 to 31 once.
All inputs are finite; a program needn't handle non-finite values.
Results may differ from a plain program's by a relative error of at most 0.015.
Values may be sent and summed in bfloat16 or wider, within the bound.
No kernel may reach another device: no remote copies, remote signals or barrier semaphores. Data moves between devices by JAX's collectives and lax.ppermute only.
A program may use at most 64 MiB of HBM per device.

v0:
```python
import jax
import jax.numpy as jnp
from jax import lax
from jax.sharding import PartitionSpec as P

logit_scale = 20.0


def tile_scores(query_rows, passage_rows):
    return logit_scale * lax.dot_general(
        query_rows, passage_rows, (((1,), (1,)), ((), ())), preferred_element_type=jnp.float32
    )


def local(query, passage, positive):
    shard_rows = query.shape[0]
    row_devices = lax.axis_size("row")
    col_devices = lax.axis_size("col")
    passage_all = lax.all_gather(passage, "row", axis=0, tiled=True)
    query_all = lax.all_gather(query, "col", axis=0, tiled=True)
    scores = tile_scores(query_all, passage_all)
    row_local_peak = scores.max(axis=1)
    col_local_peak = scores.max(axis=0)
    row_peak = lax.pmax(row_local_peak, "col")
    col_peak = lax.pmax(col_local_peak, "row")
    row_sum = lax.psum(jnp.exp(scores - row_peak[:, None]).sum(axis=1), "col")
    col_sum = lax.psum(jnp.exp(scores - col_peak[None, :]).sum(axis=0), "row")
    row_lse = row_peak + jnp.log(row_sum)
    col_lse = col_peak + jnp.log(col_sum)
    weights = (
        0.5 * (jnp.exp(scores - row_lse[:, None]) + jnp.exp(scores - col_lse[None, :]))
    ).astype(jnp.bfloat16)
    query_sum = lax.psum_scatter(
        jnp.dot(weights, passage_all, preferred_element_type=jnp.float32).astype(jnp.bfloat16),
        "col",
        scatter_dimension=0,
        tiled=True,
    ).astype(jnp.float32)
    passage_sum = lax.psum_scatter(
        lax.dot_general(
            weights, query_all, (((0,), (0,)), ((), ())), preferred_element_type=jnp.float32
        ).astype(jnp.bfloat16),
        "row",
        scatter_dimension=0,
        tiled=True,
    ).astype(jnp.float32)
    slot_index = jnp.arange(shard_rows, dtype=jnp.int32)
    onehot = (positive[0][:, None] == slot_index[None, :]).astype(jnp.bfloat16)
    paired_passage = jnp.dot(onehot, passage, preferred_element_type=jnp.float32)
    paired_query = lax.dot_general(
        onehot, query, (((0,), (0,)), ((), ())), preferred_element_type=jnp.float32
    )
    positive_score = logit_scale * jnp.sum(query.astype(jnp.float32) * paired_passage, axis=1)
    grad_query = (logit_scale * (query_sum - paired_passage)).astype(jnp.bfloat16)
    grad_passage = (logit_scale * (passage_sum - paired_query)).astype(jnp.bfloat16)
    row_part = lax.dynamic_slice_in_dim(row_lse, lax.axis_index("col") * shard_rows, shard_rows)
    col_part = lax.dynamic_slice_in_dim(col_lse, lax.axis_index("row") * shard_rows, shard_rows)
    local_terms = jnp.sum(row_part) + jnp.sum(col_part) - 2.0 * jnp.sum(positive_score)
    summed = lax.psum(local_terms, ("row", "col"))
    loss_value = summed / (2.0 * shard_rows * row_devices * col_devices)
    return (loss_value, grad_query, grad_passage)


def solution(mesh):
    return jax.shard_map(
        local,
        mesh=mesh,
        in_specs=(P(("row", "col"), None), P(("row", "col"), None), P(("row", "col"), None)),
        out_specs=(P(), P(("row", "col"), None), P(("row", "col"), None)),
        check_vma=False,
    )
```

profile of v0, /device:TPU:1, one launch (start us, length us, event | category | flops | bytes accessed | tf_op | source)
XLA Modules:
  0.0 658.9 jit_solution(3152972070807338193)
XLA Ops:
  7.2 0.0 all-gather.5.cloned.1.call-start
  7.2 0.7 all-gather.5.cloned.1.call-update
  7.9 0.0 all-gather.3.cloned.1.call-start
  7.9 0.7 all-gather.3.cloned.1.call-update
  8.6 0.0 reduce-scatter.3.cloned.1.call-start
  8.7 64.2 %all-gather.5.cloned.1.call-done = bf16[512,1024]{1,0:T(8,128)(2,1)} async-done(((bf16[32,1024]{1,0:T(8,128)(2,1)}), bf16[512,1024]{1,0:T(8,128)(2,1)}) %all-gather.5.cloned.1.call-update) | async-done | bytes 1048592 | tf_op jit(solution)/shard_map/all_gather | solution.py:19
  72.9 69.4 %all-gather.3.cloned.1.call-done = bf16[1024,1024]{1,0:T(8,128)(2,1)} async-done(((bf16[32,1024]{1,0:T(8,128)(2,1)}), bf16[1024,1024]{1,0:T(8,128)(2,1)}) %all-gather.3.cloned.1.call-update) | async-done | bytes 2097168 | tf_op jit(solution)/shard_map/all_gather | solution.py:20
  142.3 3.2 fusion.5
  145.5 37.5 %pmax.15 = f32[512]{0:T(512)S(1)} all-reduce(f32[512]{0:T(512)S(1)} %get-tuple-element.5), channel_id=1, replica_groups=mesh['row'=16,'col'=32] {'row'}, use_global_device_ids=true, to_apply=%region_6.0 | all-reduce | flops 512 | bytes 4096 | tf_op jit(solution)/shard_map/pmax | solution.py:25
  183.0 59.6 %pmax.14 = f32[1024]{0:T(1024)S(1)} all-reduce(f32[1024]{0:T(1024)S(1)} %get-tuple-element.6), channel_id=1, replica_groups=mesh['row'=16,'col'=32] {'col'}, use_global_device_ids=true, to_apply=%region_1.0 | all-reduce | flops 1024 | bytes 8192 | tf_op jit(solution)/shard_map/pmax | solution.py:24
  242.6 1.0 exponential_reduce_fusion
  243.5 32.1 %psum.22 = f32[512]{0:T(512)S(1)} all-reduce(f32[512]{0:T(512)S(1)} %get-tuple-element.3), channel_id=1, replica_groups=mesh['row'=16,'col'=32] {'row'}, use_global_device_ids=true, to_apply=%region_8.0 | all-reduce | flops 512 | bytes 4096 | tf_op jit(solution)/shard_map/psum | solution.py:27
  275.7 59.9 %psum.21 = f32[1024]{0:T(1024)S(1)} all-reduce(f32[1024]{0:T(1024)S(1)} %get-tuple-element.4), channel_id=1, replica_groups=mesh['row'=16,'col'=32] {'col'}, use_global_device_ids=true, to_apply=%region_3.0 | all-reduce | flops 1024 | bytes 8192 | tf_op jit(solution)/shard_map/psum | solution.py:26
  335.6 0.0 copy-done.3
  335.6 2.9 convolution_convert_fusion
  338.5 0.0 reduce-scatter.3.cloned.1.call-update
  338.5 0.0 copy-start
  338.5 0.0 copy-start.1
  338.5 0.0 copy-start.2
  338.5 0.0 reduce-scatter.5.cloned.1.call-start
  338.6 4.0 convolution_convert_fusion.1
  342.6 0.0 reduce-scatter.5.cloned.1.call-update
  342.6 0.7 dynamic-slice_reduce_fusion
  343.3 0.7 dynamic-slice_reduce_fusion.1
  345.3 109.5 %reduce-scatter.3.cloned.1.call-done = bf16[32,1024]{1,0:T(8,128)(2,1)} async-done(((bf16[1024,1024]{1,0:T(8,128)(2,1)}), bf16[32,1024]{1,0:T(8,128)(2,1)}) %reduce-scatter.3.cloned.1.call-update) | async-done | bytes 65552 | tf_op jit(solution)/shard_map/reduce_scatter | solution.py:33
  454.8 0.0 copy-done
  454.8 0.0 copy-done.1
  454.8 1.8 multiply_convert_fusion.1
  456.6 0.6 multiply_reduce_fusion.1
  457.8 92.4 %reduce-scatter.5.cloned.1.call-done = bf16[32,1024]{1,0:T(8,128)(2,1)} async-done(((bf16[512,1024]{1,0:T(8,128)(2,1)}), bf16[32,1024]{1,0:T(8,128)(2,1)}) %reduce-scatter.5.cloned.1.call-update) | async-done | bytes 65552 | tf_op jit(solution)/shard_map/reduce_scatter | solution.py:39
  550.2 1.7 fusion.1
  551.9 98.7 %psum.23 = f32[]{:T(128)} all-reduce(f32[]{:T(128)S(6)} %sub.45), channel_id=1, replica_groups=mesh['row'=16,'col'=32] {'row','col'}, use_global_device_ids=true, to_apply=%region_12.0 | all-reduce | flops 1 | bytes 8 | tf_op jit(solution)/shard_map/psum | solution.py:59
  (4 shorter events, 0.0 us)
Async XLA Ops:
  7.2 65.8 %all-gather.5.cloned.1.call-start = ((), (), s32[]{:S(2)}) async-start(), calls=%async_computation.3 | async-start | bytes 1114112 | tf_op jit(solution)/shard_map/all_gather | solution.py:19
  7.9 134.4 %all-gather.3.cloned.1.call-start = ((), (), s32[]{:S(2)}) async-start(), calls=%async_computation.2 | async-start | bytes 2162688 | tf_op jit(solution)/shard_map/all_gather | solution.py:20
  8.6 446.1 %reduce-scatter.3.cloned.1.call-start = ((), (), s32[]{:S(2)}) async-start(), calls=%async_computation.4 | async-start | bytes 2162688 | tf_op jit(solution)/shard_map/reduce_scatter | solution.py:33
  145.5 190.1 %copy-start.3 = (bf16[512,1024]{1,0:T(8,128)(2,1)S(1)}, bf16[512,1024]{1,0:T(8,128)(2,1)}, u32[]{:S(2)}) copy-start(bf16[512,1024]{1,0:T(8,128)(2,1)} %all-gather.5.cloned.1.call-done) | copy-start | bytes 3145732
  338.5 116.3 %copy-start = (bf16[32,1024]{1,0:T(8,128)(2,1)S(1)}, bf16[32,1024]{1,0:T(8,128)(2,1)}, u32[]{:S(2)}) copy-start(bf16[32,1024]{1,0:T(8,128)(2,1)} %param.3) | copy-start | bytes 196612
  338.5 116.3 %copy-start.1 = (bf16[32,1024]{1,0:T(8,128)(2,1)S(1)}, bf16[32,1024]{1,0:T(8,128)(2,1)}, u32[]{:S(2)}) copy-start(bf16[32,1024]{1,0:T(8,128)(2,1)} %param.4) | copy-start | bytes 196612
  338.5 116.2 %copy-start.2 = (s32[1,32]{1,0:T(1,128)S(1)}, s32[1,32]{1,0:T(1,128)}, u32[]{:S(2)}) copy-start(s32[1,32]{1,0:T(1,128)} %param.5) | copy-start | bytes 388
  338.5 211.7 %reduce-scatter.5.cloned.1.call-start = ((), (), s32[]{:S(2)}) async-start(), calls=%async_computation.5 | async-start | bytes 1114112 | tf_op jit(solution)/shard_map/reduce_scatter | solution.py:39
Sparse Core Ops, SparseCore 0:
  11.0 61.9 all-gather.4
  75.1 67.1 all-gather.2
  338.6 116.0 reduce-scatter.2
  458.7 91.4 reduce-scatter.4
where the time goes:
time: 659 us
  waiting for transfers between devices  337 us (51%)
  blocking collectives  288 us (44%)
  between operations  17.5 us (3%)
  matrix products  13.7 us (2%)
    reduce_scatter x1, waiting for transfers between devices, local(): lax.psum_scatter(jnp.dot(weights, passage_all, preferred_element_type=jnp...  109 us
    psum x1, blocking collectives, local(): summed = lax.psum(local_terms, ('row', 'col'))  98.7 us
    reduce_scatter x1, waiting for transfers between devices, local(): lax.psum_scatter(lax.dot_general(weights, query_all, (((0,), (0,)), ((),...  92.4 us
    all_gather x1, waiting for transfers between devices, local(): query_all = lax.all_gather(query, 'col', axis=0, tiled=True)  69.4 us
    all_gather x1, waiting for transfers between devices, local(): passage_all = lax.all_gather(passage, 'row', axis=0, tiled=True)  64.2 us
    psum x1, blocking collectives, local(): row_sum = lax.psum(jnp.exp(scores - row_peak[:, None]).sum(axis=1), 'col')  59.9 us
    pmax x1, blocking collectives, local(): row_peak = lax.pmax(row_local_peak, 'col')  59.6 us
    pmax x1, blocking collectives, local(): col_peak = lax.pmax(col_local_peak, 'row')  37.5 us
  transfers between devices with their start and end apart: 4, of which 4 were waited for; matrix products, arithmetic and copies ran while one was open for 1% of the time, Pallas kernels for 0%

commit v1 on v0

--- a/solution.py
+++ b/solution.py
@@ -16,7 +16,9 @@
     shard_rows = query.shape[0]
     row_devices = lax.axis_size("row")
     col_devices = lax.axis_size("col")
-    passage_all = lax.all_gather(passage, "row", axis=0, tiled=True)
+    passage_all = jnp.concatenate(
+        lax.all_to_all(jnp.stack(lax.axis_size("row") * [passage]), "row", 0, 0), axis=0
+    )
     query_all = lax.all_gather(query, "col", axis=0, tiled=True)
     scores = tile_scores(query_all, passage_all)
     row_local_peak = scores.max(axis=1)

time: 659 us -> 602 us (0.914)
  waiting for transfers between devices: 337 us -> 240 us
  blocking collectives: 288 us -> 326 us
    all_gather x1 -> x0, waiting for transfers between devices: 64.2 us -> none  [local(): passage_all = lax.all_gather(passage, 'row', axis=0, tiled=True)]
    all_to_all x0 -> x1, blocking collectives: none -> 40 us  [local(): lax.all_to_all(jnp.stack(lax.axis_size('row') * [passage]), 'row', 0, 0)]
    all_gather x1, waiting for transfers between devices: 69.4 us -> 37.9 us  [local(): query_all = lax.all_gather(query, 'col', axis=0, tiled=True)]
  transfers between devices with their start and end apart: 4 -> 3, of which waited for: 4 -> 3; matrix products, arithmetic and copies ran while one was open for 1% -> 1% of each run, Pallas kernels for 0% -> 0%
where the time goes in v1:
time: 602 us; the launch traced here: 601 us
  blocking collectives  326 us (54%)
  waiting for transfers between devices  240 us (40%)
  between operations  17.5 us (3%)
  matrix products  13.5 us (2%)
    reduce_scatter x1, waiting for transfers between devices, local(): lax.psum_scatter(jnp.dot(weights, passage_all, preferred_element_type=jnp...  109 us
    psum x1, blocking collectives, local(): summed = lax.psum(local_terms, ('row', 'col'))  98.7 us
    reduce_scatter x1, waiting for transfers between devices, local(): lax.psum_scatter(lax.dot_general(weights, query_all, (((0,), (0,)), ((),...  92.5 us
    psum x1, blocking collectives, local(): row_sum = lax.psum(jnp.exp(scores - row_peak[:, None]).sum(axis=1), 'col')  59.9 us
    pmax x1, blocking collectives, local(): row_peak = lax.pmax(row_local_peak, 'col')  59.9 us
    all_to_all x1, blocking collectives, local(): lax.all_to_all(jnp.stack(lax.axis_size('row') * [passage]), 'row', 0, 0)  40 us
    all_gather x1, waiting for transfers between devices, local(): query_all = lax.all_gather(query, 'col', axis=0, tiled=True)  37.9 us
    pmax x1, blocking collectives, local(): col_peak = lax.pmax(col_local_peak, 'row')  35.8 us
  transfers between devices with their start and end apart: 3, of which 3 were waited for; matrix products, arithmetic and copies ran while one was open for 1% of the time, Pallas kernels for 0%

profile of v1, /device:TPU:1, one launch (start us, length us, event | category | flops | bytes accessed | tf_op | source)
XLA Modules:
  0.0 601.4 jit_solution(7661192494636350631)
XLA Ops:
  7.2 0.0 all-gather.2.cloned.1.call-start
  7.2 0.7 all-gather.2.cloned.1.call-update
  7.9 0.0 reduce-scatter.3.cloned.1.call-start
  7.9 1.0 stack.2
  8.9 40.0 %all_to_all.5 = bf16[16,32,1024]{2,1,0:T(8,128)(2,1)S(1)} all-to-all(bf16[16,32,1024]{2,1,0:T(8,128)(2,1)S(1)} %stack.2), channel_id=1, replica_groups=mesh['row'=16,'col'=32] {'row'}, dimensions={0} | all-to-all | bytes 2097152 | tf_op jit(solution)/shard_map/all_to_all | solution.py:20
  49.0 37.9 %all-gather.2.cloned.1.call-done = bf16[1024,1024]{1,0:T(8,128)(2,1)} async-done(((bf16[32,1024]{1,0:T(8,128)(2,1)}), bf16[1024,1024]{1,0:T(8,128)(2,1)}) %all-gather.2.cloned.1.call-update) | async-done | bytes 2097168 | tf_op jit(solution)/shard_map/all_gather | solution.py:22
  86.9 3.0 fusion.5
  89.8 35.8 %pmax.15 = f32[512]{0:T(512)S(1)} all-reduce(f32[512]{0:T(512)S(1)} %get-tuple-element.5), channel_id=1, replica_groups=mesh['row'=16,'col'=32] {'row'}, use_global_device_ids=true, to_apply=%region_6.0 | all-reduce | flops 512 | bytes 4096 | tf_op jit(solution)/shard_map/pmax | solution.py:27
  125.7 59.9 %pmax.14 = f32[1024]{0:T(1024)S(1)} all-reduce(f32[1024]{0:T(1024)S(1)} %get-tuple-element.6), channel_id=1, replica_groups=mesh['row'=16,'col'=32] {'col'}, use_global_device_ids=true, to_apply=%region_1.0 | all-reduce | flops 1024 | bytes 8192 | tf_op jit(solution)/shard_map/pmax | solution.py:26
  185.5 1.0 exponential_reduce_fusion
  186.5 32.1 %psum.22 = f32[512]{0:T(512)S(1)} all-reduce(f32[512]{0:T(512)S(1)} %get-tuple-element.3), channel_id=1, replica_groups=mesh['row'=16,'col'=32] {'row'}, use_global_device_ids=true, to_apply=%region_8.0 | all-reduce | flops 512 | bytes 4096 | tf_op jit(solution)/shard_map/psum | solution.py:29
  218.6 59.9 %psum.21 = f32[1024]{0:T(1024)S(1)} all-reduce(f32[1024]{0:T(1024)S(1)} %get-tuple-element.4), channel_id=1, replica_groups=mesh['row'=16,'col'=32] {'col'}, use_global_device_ids=true, to_apply=%region_3.0 | all-reduce | flops 1024 | bytes 8192 | tf_op jit(solution)/shard_map/psum | solution.py:28
  278.6 2.9 convolution_convert_fusion
  281.5 0.0 reduce-scatter.3.cloned.1.call-update
  281.5 0.0 copy-start
  281.5 0.0 copy-start.1
  281.5 0.0 copy-start.2
  281.5 0.0 reduce-scatter.5.cloned.1.call-start
  281.6 4.0 convolution_convert_fusion.1
  285.6 0.0 reduce-scatter.5.cloned.1.call-update
  285.7 0.7 dynamic-slice_reduce_fusion
  286.3 0.7 dynamic-slice_reduce_fusion.1
  288.3 108.7 %reduce-scatter.3.cloned.1.call-done = bf16[32,1024]{1,0:T(8,128)(2,1)} async-done(((bf16[1024,1024]{1,0:T(8,128)(2,1)}), bf16[32,1024]{1,0:T(8,128)(2,1)}) %reduce-scatter.3.cloned.1.call-update) | async-done | bytes 65552 | tf_op jit(solution)/shard_map/reduce_scatter | solution.py:35
  397.0 0.0 copy-done
  397.0 0.0 copy-done.1
  397.0 0.0 copy-done.2
  397.0 1.8 multiply_convert_fusion.1
  398.8 0.6 multiply_reduce_fusion.1
  400.1 92.5 %reduce-scatter.5.cloned.1.call-done = bf16[32,1024]{1,0:T(8,128)(2,1)} async-done(((bf16[512,1024]{1,0:T(8,128)(2,1)}), bf16[32,1024]{1,0:T(8,128)(2,1)}) %reduce-scatter.5.cloned.1.call-update) | async-done | bytes 65552 | tf_op jit(solution)/shard_map/reduce_scatter | solution.py:41
  492.6 1.7 fusion.1
  494.4 98.7 %psum.23 = f32[]{:T(128)} all-reduce(f32[]{:T(128)S(6)} %sub.45), channel_id=1, replica_groups=mesh['row'=16,'col'=32] {'row','col'}, use_global_device_ids=true, to_apply=%region_12.0 | all-reduce | flops 1 | bytes 8 | tf_op jit(solution)/shard_map/psum | solution.py:61
  (2 shorter events, 0.0 us)
Async XLA Ops:
  7.2 79.7 %all-gather.2.cloned.1.call-start = ((), (), s32[]{:S(2)}) async-start(), calls=%async_computation.3 | async-start | bytes 2162688 | tf_op jit(solution)/shard_map/all_gather | solution.py:22
  7.9 389.1 %reduce-scatter.3.cloned.1.call-start = ((), (), s32[]{:S(2)}) async-start(), calls=%async_computation.4 | async-start | bytes 2162688 | tf_op jit(solution)/shard_map/reduce_scatter | solution.py:35
  281.5 115.5 %copy-start = (bf16[32,1024]{1,0:T(8,128)(2,1)S(1)}, bf16[32,1024]{1,0:T(8,128)(2,1)}, u32[]{:S(2)}) copy-start(bf16[32,1024]{1,0:T(8,128)(2,1)} %param.3) | copy-start | bytes 196612
  281.5 115.5 %copy-start.1 = (bf16[32,1024]{1,0:T(8,128)(2,1)S(1)}, bf16[32,1024]{1,0:T(8,128)(2,1)}, u32[]{:S(2)}) copy-start(bf16[32,1024]{1,0:T(8,128)(2,1)} %param.4) | copy-start | bytes 196612
  281.5 115.5 %copy-start.2 = (s32[1,32]{1,0:T(1,128)S(1)}, s32[1,32]{1,0:T(1,128)}, u32[]{:S(2)}) copy-start(s32[1,32]{1,0:T(1,128)} %param.5) | copy-start | bytes 388
  281.5 211.1 %reduce-scatter.5.cloned.1.call-start = ((), (), s32[]{:S(2)}) async-start(), calls=%async_computation.5 | async-start | bytes 1114112 | tf_op jit(solution)/shard_map/reduce_scatter | solution.py:41
Sparse Core Ops, SparseCore 0:
  10.1 76.7 all-gather.1
  281.6 115.3 reduce-scatter.2
  401.1 91.4 reduce-scatter.4
